TPU v7x, 256 devices: a whole 4x4x8 slice. The times are simulated.
256 devices in a mesh: row: 32 (over x, y, core), col: 8 (over z).
Axes of the slice: x: 4, y: 4, z: 8, core: 2. Of those that a mesh axis runs over, the one named last changes fastest.
Arguments:
- block_values: bfloat16 [32, 8, 192, 128, 128], P('row', 'col'), may hold values from -0.0625 to 0.0625
- block_rows: int32 [32, 8, 192], P('row', 'col'), may hold values from 0 to 4095, as said below
- block_cols: int32 [32, 8, 192], P('row', 'col'), may hold values from 0 to 4095, as said below
- block_counts: int32 [32, 8], P('row', 'col'), may hold values from 48 to 192, as said below
- precond: float32 [8, 512, 128, 128], P('col', 'row')
- right_side: float32 [8, 512, 32, 128], P('col', 'row'), may hold values from -6 to 6
Outputs:
- solution: float32 [8, 512, 32, 128], P('col', 'row')
Inputs may be any that keep to these rules, and one draw needn't show every extreme that they name: `block_rows`: the block rows of device (r, c) lie in [c * 512, (c + 1) * 512); positions may repeat; for each j, at most 9 of a device's 192 slots have (row mod 512) // 16 == j, and in every index of col some j has exactly 9 such slots on every device. `block_cols`: every block column q of device (r, c) has (q mod 512) // 16 == r; positions may repeat. `block_counts`: slots at or past a device's count are unused; some device uses all 192 slots.
All inputs are finite; a program needn't handle non-finite values.
Results may differ from a plain program's by a relative error of at most 0.00073.
Values may be sent and summed in bfloat16 or wider, within the bound.
A program may use at most 64 MiB of HBM per device.

v0:
```python
import jax
import jax.numpy as jnp
from jax import lax
from jax.sharding import PartitionSpec as P

ITERS = 3


def apply_blocks(matrix, field):
    return jnp.einsum("poi,pki->pko", matrix, field, precision=lax.Precision.HIGHEST)


def block_terms(vectors, values, col_local):
    gathered = vectors[col_local]
    return jnp.einsum("ski,soi->sko", gathered, values, preferred_element_type=jnp.float32)


def per_device(block_values, block_rows, block_cols, block_counts, precond, right_side):
    owned = right_side.shape[1]
    row_devices = lax.axis_size("row")
    group = owned * row_devices
    slot_total = block_values.shape[2]
    values = block_values[0, 0]
    row_local = block_rows[0, 0] % group
    col_global = block_cols[0, 0]
    col_local = col_global // group * owned + col_global % owned
    used = block_counts[0, 0]
    live = jnp.arange(slot_total, dtype=jnp.int32) < used
    inverse = precond[0]
    rhs_own = right_side[0]
    solution = apply_blocks(inverse, rhs_own)
    for step in range(ITERS):
        pieces = lax.all_gather(solution.astype(jnp.bfloat16)[None], "col", axis=1, tiled=True)[0]
        terms = block_terms(pieces, values, col_local)
        terms = jnp.where(live[:, None, None], terms, jnp.zeros_like(terms))
        partial_value = jax.ops.segment_sum(terms, row_local, num_segments=group)
        product = lax.psum_scatter(partial_value, "row", scatter_dimension=0, tiled=True)
        residual = rhs_own - solution - product
        solution = solution + apply_blocks(inverse, residual)
    return solution[None]


def solution(mesh):
    placed = (
        P("row", "col", None, None, None),
        P("row", "col", None),
        P("row", "col", None),
        P("row", "col"),
        P("col", "row", None, None),
        P("col", "row", None, None),
    )
    return jax.shard_map(
        per_device,
        mesh=mesh,
        in_specs=placed,
        out_specs=P("col", "row", None, None),
        check_vma=False,
    )
```

profile of v0, /device:TPU:2, one launch (start us, length us, event | category | flops | bytes accessed | tf_op | source)
XLA Modules:
  0.0 562.6 jit_solution(1981962366836233417)
XLA Ops:
  6.5 1.2 copy-done
  7.8 3.3 fusion.30
  11.1 0.0 all-gather.7.cloned.1.call-update
  11.1 0.0 reduce-scatter.4.cloned.1.call-start
  11.8 0.7 compare_select_fusion
  12.5 0.7 and_select_fusion.2
  13.2 39.4 %all-gather.7.cloned.1.call-done = bf16[128,32,128]{2,1,0:T(8,128)(2,1)} async-done(((bf16[16,32,128]{2,1,0:T(8,128)(2,1)}), bf16[128,32,128]{2,1,0:T(8,128)(2,1)}) %all-gather.7.cloned.1.call-update) | async-done | bytes 1048592 | tf_op jit(solution)/shard_map/all_gather | solution.py:33
  52.6 2.1 gather_fusion
  54.8 7.9 %fusion.6 = f32[192,32,128]{2,1,0:T(8,128)} fusion(bf16[192,32,128]{2,1,0:T(8,128)(2,1)S(1)} %gather_fusion, bf16[1,1,192,128,128]{4,3,2,1,0:T(8,128)(2,1)} %param.6, pred[192]{0:T(512)(128)(4,1)S(1)} %iota_compare_fusion), kind=kOutput, calls=%fused_computation.12 | convolution fusion | flops 202113024 | bytes 11010240 | tf_op jit(solution)/shard_map/ski,soi->sko/dot_general | solution.py:15
  62.7 4.3 broadcast.156.clone
  67.0 25.8 %scatter_fusion = f32[512,32,128]{2,1,0:T(8,128)} fusion(f32[512,32,128]{2,1,0:T(8,128)} %broadcast.156.clone, s32[192]{0:T(256)S(1)} %bitcast.73, f32[192,32,128]{2,1,0:T(8,128)} %fusion.6), kind=kCustom, calls=%fused_computation.3 | custom fusion | flops 786432 | bytes 9437952 | tf_op jit(solution)/shard_map/scatter-add | solution.py:36
  92.9 0.0 all-gather.9.cloned.1.call-start
  92.9 98.6 %reduce-scatter.4.cloned.1.call-done = f32[16,32,128]{2,1,0:T(8,128)} async-done(((f32[512,32,128]{2,1,0:T(8,128)}), f32[16,32,128]{2,1,0:T(8,128)}) %reduce-scatter.4.cloned.1.call-update) | async-done | bytes 262160 | tf_op jit(solution)/shard_map/reduce_scatter | solution.py:37
  191.5 3.3 fusion.31
  194.8 0.0 all-gather.9.cloned.1.call-update
  194.8 0.0 reduce-scatter.6.cloned.1.call-start
  194.9 38.2 %all-gather.9.cloned.1.call-done = bf16[128,32,128]{2,1,0:T(8,128)(2,1)} async-done(((bf16[16,32,128]{2,1,0:T(8,128)(2,1)}), bf16[128,32,128]{2,1,0:T(8,128)(2,1)}) %all-gather.9.cloned.1.call-update) | async-done | bytes 1048592 | tf_op jit(solution)/shard_map/all_gather | solution.py:33
  233.1 2.1 gather_fusion.1
  235.2 7.9 %fusion.9 = f32[192,32,128]{2,1,0:T(8,128)} fusion(bf16[192,32,128]{2,1,0:T(8,128)(2,1)S(1)} %gather_fusion.1, bf16[1,1,192,128,128]{4,3,2,1,0:T(8,128)(2,1)} %param.6, pred[192]{0:T(512)(128)(4,1)S(1)} %iota_compare_fusion), kind=kOutput, calls=%fused_computation.13 | convolution fusion | flops 202113024 | bytes 11010240 | tf_op jit(solution)/shard_map/ski,soi->sko/dot_general | solution.py:15
  243.1 4.3 broadcast.156.clone.1
  247.4 25.8 %scatter_fusion.1 = f32[512,32,128]{2,1,0:T(8,128)} fusion(f32[512,32,128]{2,1,0:T(8,128)} %broadcast.156.clone.1, s32[192]{0:T(256)S(1)} %bitcast.74, f32[192,32,128]{2,1,0:T(8,128)} %fusion.9), kind=kCustom, calls=%fused_computation.4 | custom fusion | flops 786432 | bytes 9437952 | tf_op jit(solution)/shard_map/scatter-add | solution.py:36
  273.3 0.0 all-gather.11.cloned.1.call-start
  273.4 98.6 %reduce-scatter.6.cloned.1.call-done = f32[16,32,128]{2,1,0:T(8,128)} async-done(((f32[512,32,128]{2,1,0:T(8,128)}), f32[16,32,128]{2,1,0:T(8,128)}) %reduce-scatter.6.cloned.1.call-update) | async-done | bytes 262160 | tf_op jit(solution)/shard_map/reduce_scatter | solution.py:37
  371.9 3.3 fusion.32
  375.3 0.2 reduce-scatter.8.cloned.1.call-start
  375.5 38.0 %all-gather.11.cloned.1.call-done = bf16[128,32,128]{2,1,0:T(8,128)(2,1)} async-done(((bf16[16,32,128]{2,1,0:T(8,128)(2,1)}), bf16[128,32,128]{2,1,0:T(8,128)(2,1)}) %all-gather.11.cloned.1.call-update) | async-done | bytes 1048592 | tf_op jit(solution)/shard_map/all_gather | solution.py:33
  413.6 2.1 gather_fusion.2
  415.7 7.9 %fusion.12 = f32[192,32,128]{2,1,0:T(8,128)} fusion(bf16[192,32,128]{2,1,0:T(8,128)(2,1)S(1)} %gather_fusion.2, bf16[1,1,192,128,128]{4,3,2,1,0:T(8,128)(2,1)} %param.6, pred[192]{0:T(512)(128)(4,1)S(1)} %iota_compare_fusion), kind=kOutput, calls=%fused_computation.14 | convolution fusion | flops 202113024 | bytes 11010240 | tf_op jit(solution)/shard_map/ski,soi->sko/dot_general | solution.py:15
  423.6 4.3 broadcast.156
  427.9 25.8 %scatter_fusion.2 = f32[512,32,128]{2,1,0:T(8,128)} fusion(f32[512,32,128]{2,1,0:T(8,128)} %broadcast.156, s32[192]{0:T(256)S(1)} %bitcast.75, f32[192,32,128]{2,1,0:T(8,128)} %fusion.12), kind=kCustom, calls=%fused_computation.5 | custom fusion | flops 786432 | bytes 9437952 | tf_op jit(solution)/shard_map/scatter-add | solution.py:36
  453.8 98.6 %reduce-scatter.8.cloned.1.call-done = f32[16,32,128]{2,1,0:T(8,128)} async-done(((f32[512,32,128]{2,1,0:T(8,128)}), f32[16,32,128]{2,1,0:T(8,128)}) %reduce-scatter.8.cloned.1.call-update) | async-done | bytes 262160 | tf_op jit(solution)/shard_map/reduce_scatter | solution.py:37
  552.4 3.4 fusion.15
  (10 shorter events, 0.1 us)
Async XLA Ops:
  6.5 1.2 copy-start
  6.5 46.1 %all-gather.7.cloned.1.call-start = ((), (), s32[]{:S(2)}) async-start(), calls=%async_computation.6 | async-start | bytes 1179648 | tf_op jit(solution)/shard_map/all_gather | solution.py:33
  11.1 180.3 %reduce-scatter.4.cloned.1.call-start = ((), (), s32[]{:S(2)}) async-start(), calls=%async_computation.3 | async-start | bytes 8650752 | tf_op jit(solution)/shard_map/reduce_scatter | solution.py:37
  92.8 98.7 %copy-start.1 = (f32[1,16,32,128]{3,2,1,0:T(8,128)S(1)}, f32[1,16,32,128]{3,2,1,0:T(8,128)}, u32[]{:S(2)}) copy-start(f32[1,16,32,128]{3,2,1,0:T(8,128)} %param.11) | copy-start | bytes 786436
  92.9 140.3 %all-gather.9.cloned.1.call-start = ((), (), s32[]{:S(2)}) async-start(), calls=%async_computation.7 | async-start | bytes 1179648 | tf_op jit(solution)/shard_map/all_gather | solution.py:33
  194.8 177.1 %reduce-scatter.6.cloned.1.call-start = ((), (), s32[]{:S(2)}) async-start(), calls=%async_computation.4 | async-start | bytes 8650752 | tf_op jit(solution)/shard_map/reduce_scatter | solution.py:37
  273.3 140.3 %all-gather.11.cloned.1.call-start = ((), (), s32[]{:S(2)}) async-start(), calls=%async_computation.8 | async-start | bytes 1179648 | tf_op jit(solution)/shard_map/all_gather | solution.py:33
  375.3 177.1 %reduce-scatter.8.cloned.1.call-start = ((), (), s32[]{:S(2)}) async-start(), calls=%async_computation.5 | async-start | bytes 8650752 | tf_op jit(solution)/shard_map/reduce_scatter | solution.py:37
Sparse Core Ops, SparseCore 0:
  11.2 41.3 all-gather.6
  93.0 98.4 reduce-scatter.3
  195.0 38.0 all-gather.8
  273.4 98.4 reduce-scatter.5
  375.4 38.0 all-gather.10
  453.9 98.4 reduce-scatter.7
where the time goes:
time: 564 us; the launch traced here: 563 us
  waiting for transfers between devices  412 us (73%)
  other arithmetic  78.9 us (14%)
  matrix products  37.1 us (7%)
  local copies, waits for them, and re-layouts  20.5 us (4%)
  between operations  14.2 us (3%)
    reduce_scatter x3, waiting for transfers between devices, per_device(): lax.psum_scatter(partial_value, 'row', scatter_dimension=0, tiled=True)  296 us
    all_gather x3, waiting for transfers between devices, per_device(): lax.all_gather(solution.astype(jnp.bfloat16)[None], 'col', axis=1, tiled=...  116 us
    scatter-add x3, other arithmetic, per_device(): partial_value = jax.ops.segment_sum(terms, row_local, num_segments=group)  77.5 us
    dot_general x3, matrix products, block_terms(): jnp.einsum('ski,soi->sko', gathered, values, preferred_element_type=jnp.f...  23.7 us
    dot_general x4, matrix products, apply_blocks(): jnp.einsum('poi,pki->pko', matrix, field, precision=lax.Precision.HIGHEST)  13.4 us
    another operation x3, local copies, waits for them, and re-layouts  12.9 us
  transfers between devices with their start and end apart: 6, of which 6 were waited for; matrix products, arithmetic and copies ran while one was open for 0% of the time, Pallas kernels for 0%

commit v1 on v0

--- a/solution.py
+++ b/solution.py
@@ -4,6 +4,28 @@
 from jax.sharding import PartitionSpec as P
 
 ITERS = 3
+
+
+def laid_out(blocks, dim):
+    shape = list(blocks.shape[1:])
+    shape[dim] *= blocks.shape[0]
+    return jnp.moveaxis(blocks, 0, dim).reshape(shape)
+
+
+def collect(value, axis, dim):
+    size = lax.axis_size(axis)
+    pairs = [(i, (i + 1) % size) for i in range(size)]
+    back = [(b, a) for a, b in pairs]
+    lower, upper = ([], [])
+    for lap in range(size - 1):
+        if lap % 2 == 0:
+            lower.append(lax.ppermute(lower[-1] if lower else value, axis, pairs))
+        else:
+            upper.append(lax.ppermute(upper[-1] if upper else value, axis, back))
+    blocks = jnp.stack([*lower[::-1], value, *upper])
+    shift = lax.axis_index(axis) - len(lower)
+    blocks = blocks[(jnp.arange(size) - shift) % size]
+    return laid_out(blocks, dim)
 
 
 def apply_blocks(matrix, field):
@@ -30,7 +52,7 @@
     rhs_own = right_side[0]
     solution = apply_blocks(inverse, rhs_own)
     for step in range(ITERS):
-        pieces = lax.all_gather(solution.astype(jnp.bfloat16)[None], "col", axis=1, tiled=True)[0]
+        pieces = collect(solution.astype(jnp.bfloat16)[None], "col", 1)[0]
         terms = block_terms(pieces, values, col_local)
         terms = jnp.where(live[:, None, None], terms, jnp.zeros_like(terms))
         partial_value = jax.ops.segment_sum(terms, row_local, num_segments=group)

time: 564 us -> 539 us (0.956)
  waiting for transfers between devices: 412 us -> 345 us
  starting transfers between devices: 0.39 us -> 36.1 us
  local copies, waits for them, and re-layouts: 20.5 us -> 27.2 us
    all_gather x3 -> x0, waiting for transfers between devices: 116 us -> none  [per_device(): lax.all_gather(solution.astype(jnp.bfloat16)[None], 'col', axis=1, tiled=...]
    ppermute x0 -> x21, waiting for transfers between devices: none -> 43.3 us  [the longest x12 42.4 us: collect(): lower.append(lax.ppermute(lower[-1] if lower else value, axis, pairs))]
    ppermute x0 -> x21, starting transfers between devices: none -> 36 us  [the longest x9 29.1 us: collect(): upper.append(lax.ppermute(upper[-1] if upper else value, axis, back))]
    reduce_scatter x3, waiting for transfers between devices: 296 us -> 302 us  [per_device(): lax.psum_scatter(partial_value, 'row', scatter_dimension=0, tiled=True)]
    another operation x3 -> x6, local copies, waits for them, and re-layouts: 12.9 us -> 13 us
  transfers between devices with their start and end apart: 6 -> 24, of which waited for: 6 -> 19; matrix products, arithmetic and copies ran while one was open for 0% -> 0% of each run, Pallas kernels for 0% -> 0%
where the time goes in v1:
time: 539 us; the launch traced here: 538 us
  waiting for transfers between devices  345 us (64%)
  other arithmetic  79.1 us (15%)
  matrix products  36.6 us (7%)
  starting transfers between devices  36.1 us (7%)
  local copies, waits for them, and re-layouts  27.2 us (5%)
  between operations  14.1 us (3%)
    reduce_scatter x3, waiting for transfers between devices, per_device(): lax.psum_scatter(partial_value, 'row', scatter_dimension=0, tiled=True)  302 us
    scatter-add x3, other arithmetic, per_device(): partial_value = jax.ops.segment_sum(terms, row_local, num_segments=group)  77.5 us
    ppermute x12, waiting for transfers between devices, collect(): lower.append(lax.ppermute(lower[-1] if lower else value, axis, pairs))  42.4 us
    ppermute x9, starting transfers between devices, collect(): upper.append(lax.ppermute(upper[-1] if upper else value, axis, back))  29.1 us
    dot_general x3, matrix products, block_terms(): jnp.einsum('ski,soi->sko', gathered, values, preferred_element_type=jnp.f...  25.2 us
    another operation x3, local copies, waits for them, and re-layouts  12.9 us
    dot_general x4, matrix products, apply_blocks(): jnp.einsum('poi,pki->pko', matrix, field, precision=lax.Precision.HIGHEST)  11.4 us
  transfers between devices with their start and end apart: 24, of which 19 were waited for; matrix products, arithmetic and copies ran while one was open for 0% of the time, Pallas kernels for 0%

profile of v1, /device:TPU:2, one launch (start us, length us, event | category | flops | bytes accessed | tf_op | source)
XLA Modules:
  0.0 538.2 jit_solution(18275011482617165357)
XLA Ops:
  12.5 4.0 collective-permute-start.4
  17.2 2.7 collective-permute-done
  20.6 5.5 %collective-permute-done.1 = bf16[1,16,32,128]{3,2,1,0:T(8,128)(2,1)S(1)} collective-permute-done((bf16[1,16,32,128]{3,2,1,0:T(8,128)(2,1)S(1)}, bf16[1,16,32,128]{3,2,1,0:T(8,128)(2,1)S(1)}, u32[]{:S(2)}, u32[]{:S(2)}) %collective-permute-start.1) | collective-permute-done | bytes 131104 | tf_op jit(solution)/shard_map/ppermute | solution.py:22
  26.8 3.3 collective-permute-start.5
  32.6 3.7 collective-permute-start.6
  41.6 8.4 %fusion.6 = f32[192,32,128]{2,1,0:T(8,128)} fusion(bf16[192,32,128]{2,1,0:T(8,128)(2,1)} %gather_fusion.1, bf16[1,1,192,128,128]{4,3,2,1,0:T(8,128)(2,1)} %param.6, pred[192]{0:T(512)(128)(4,1)S(1)} %iota_compare_fusion), kind=kOutput, calls=%fused_computation.15 | convolution fusion | flops 202113024 | bytes 11010240 | tf_op jit(solution)/shard_map/ski,soi->sko/dot_general | solution.py:37
  50.0 4.3 broadcast.221.clone
  54.3 25.8 %scatter_fusion = f32[512,32,128]{2,1,0:T(8,128)} fusion(f32[512,32,128]{2,1,0:T(8,128)} %broadcast.221.clone, s32[192]{0:T(256)S(1)} %bitcast.129, f32[192,32,128]{2,1,0:T(8,128)} %fusion.6), kind=kCustom, calls=%fused_computation.6 | custom fusion | flops 786432 | bytes 9437952 | tf_op jit(solution)/shard_map/scatter-add | solution.py:58
  80.2 101.2 %reduce-scatter.4.cloned.1.call-done = f32[16,32,128]{2,1,0:T(8,128)} async-done(((f32[512,32,128]{2,1,0:T(8,128)}), f32[16,32,128]{2,1,0:T(8,128)}) %reduce-scatter.4.cloned.1.call-update) | async-done | bytes 262160 | tf_op jit(solution)/shard_map/reduce_scatter | solution.py:59
  181.4 2.7 convolution_add_fusion.2
  185.9 4.7 collective-permute-done.7
  193.9 3.4 collective-permute-done.8
  197.4 3.3 collective-permute-start.12
  200.8 3.9 collective-permute-done.9
  204.6 3.2 collective-permute-start.13
  207.9 2.9 collective-permute-done.10
  216.0 8.4 %fusion.9 = f32[192,32,128]{2,1,0:T(8,128)} fusion(bf16[192,32,128]{2,1,0:T(8,128)(2,1)} %gather_fusion.3, bf16[1,1,192,128,128]{4,3,2,1,0:T(8,128)(2,1)} %param.6, pred[192]{0:T(512)(128)(4,1)S(1)} %iota_compare_fusion), kind=kOutput, calls=%fused_computation.16 | convolution fusion | flops 202113024 | bytes 11010240 | tf_op jit(solution)/shard_map/ski,soi->sko/dot_general | solution.py:37
  224.4 4.3 broadcast.221.clone.1
  228.7 25.8 %scatter_fusion.1 = f32[512,32,128]{2,1,0:T(8,128)} fusion(f32[512,32,128]{2,1,0:T(8,128)} %broadcast.221.clone.1, s32[192]{0:T(256)S(1)} %bitcast.130, f32[192,32,128]{2,1,0:T(8,128)} %fusion.9), kind=kCustom, calls=%fused_computation.7 | custom fusion | flops 786432 | bytes 9437952 | tf_op jit(solution)/shard_map/scatter-add | solution.py:58
  254.6 100.3 %reduce-scatter.6.cloned.1.call-done = f32[16,32,128]{2,1,0:T(8,128)} async-done(((f32[512,32,128]{2,1,0:T(8,128)}), f32[16,32,128]{2,1,0:T(8,128)}) %reduce-scatter.6.cloned.1.call-update) | async-done | bytes 262160 | tf_op jit(solution)/shard_map/reduce_scatter | solution.py:59
  354.9 2.7 convolution_add_fusion.1
  359.3 4.7 collective-permute-done.14
  367.2 3.4 collective-permute-done.15
  370.8 3.3 collective-permute-start.19
  374.2 3.9 collective-permute-done.16
  378.0 3.2 collective-permute-start.20
  381.3 2.9 collective-permute-done.17
  389.4 8.4 %fusion.12 = f32[192,32,128]{2,1,0:T(8,128)} fusion(bf16[192,32,128]{2,1,0:T(8,128)(2,1)} %gather_fusion.5, bf16[1,1,192,128,128]{4,3,2,1,0:T(8,128)(2,1)} %param.6, pred[192]{0:T(512)(128)(4,1)S(1)} %iota_compare_fusion), kind=kOutput, calls=%fused_computation.17 | convolution fusion | flops 202113024 | bytes 11010240 | tf_op jit(solution)/shard_map/ski,soi->sko/dot_general | solution.py:37
  397.8 4.3 broadcast.221
  402.1 25.8 %scatter_fusion.2 = f32[512,32,128]{2,1,0:T(8,128)} fusion(f32[512,32,128]{2,1,0:T(8,128)} %broadcast.221, s32[192]{0:T(256)S(1)} %bitcast.131, f32[192,32,128]{2,1,0:T(8,128)} %fusion.12), kind=kCustom, calls=%fused_computation.8 | custom fusion | flops 786432 | bytes 9437952 | tf_op jit(solution)/shard_map/scatter-add | solution.py:58
  428.0 100.3 %reduce-scatter.8.cloned.1.call-done = f32[16,32,128]{2,1,0:T(8,128)} async-done(((f32[512,32,128]{2,1,0:T(8,128)}), f32[16,32,128]{2,1,0:T(8,128)}) %reduce-scatter.8.cloned.1.call-update) | async-done | bytes 262160 | tf_op jit(solution)/shard_map/reduce_scatter | solution.py:59
  528.3 3.4 fusion.15
  (79 shorter events, 35.8 us)
Async XLA Ops:
  6.5 1.2 copy-start
  6.5 174.9 %reduce-scatter.4.cloned.1.call-start = ((), (), s32[]{:S(2)}) async-start(), calls=%async_computation.3 | async-start | bytes 8650752 | tf_op jit(solution)/shard_map/reduce_scatter | solution.py:59
  10.5 9.4 %collective-permute-start = (bf16[1,16,32,128]{3,2,1,0:T(8,128)(2,1)S(1)}, bf16[1,16,32,128]{3,2,1,0:T(8,128)(2,1)S(1)}, u32[]{:S(2)}, u32[]{:S(2)}) collective-permute-start(bf16[1,16,32,128]{3,2,1,0:T(8,128)(2,1)S(1)} %convert_bitcast_fusion.2), channel_id=1, source_target_pairs={{0,1},{1,2},{2,3},{3,4},{4,5},{5,6},{6,7},{7,0},{8,9},{9,10},{10,1... | collective-permute-start | bytes 393224 | tf_op jit(solution)/shard_map/ppermute | solution.py:22
  12.5 14.3 %collective-permute-start.4 = (bf16[1,16,32,128]{3,2,1,0:T(8,128)(2,1)S(1)}, bf16[1,16,32,128]{3,2,1,0:T(8,128)(2,1)S(1)}, u32[]{:S(2)}, u32[]{:S(2)}) collective-permute-start(bf16[1,16,32,128]{3,2,1,0:T(8,128)(2,1)S(1)} %convert_bitcast_fusion.2), channel_id=1, source_target_pairs={{1,0},{2,1},{3,2},{4,3},{5,4},{6,5},{7,6},{0,7},{9,8},{10,9},{11,1... | collective-permute-start | bytes 393224 | tf_op jit(solution)/shard_map/ppermute | solution.py:24
  19.9 6.2 %collective-permute-start.1 = (bf16[1,16,32,128]{3,2,1,0:T(8,128)(2,1)S(1)}, bf16[1,16,32,128]{3,2,1,0:T(8,128)(2,1)S(1)}, u32[]{:S(2)}, u32[]{:S(2)}) collective-permute-start(bf16[1,16,32,128]{3,2,1,0:T(8,128)(2,1)S(1)} %collective-permute-done), channel_id=1, source_target_pairs={{0,1},{1,2},{2,3},{3,4},{4,5},{5,6},{6,7},{7,0},{8,9},{9,10},{10,1... | collective-permute-start | bytes 393224 | tf_op jit(solution)/shard_map/ppermute | solution.py:22
  26.1 6.2 %collective-permute-start.2 = (bf16[1,16,32,128]{3,2,1,0:T(8,128)(2,1)S(1)}, bf16[1,16,32,128]{3,2,1,0:T(8,128)(2,1)S(1)}, u32[]{:S(2)}, u32[]{:S(2)}) collective-permute-start(bf16[1,16,32,128]{3,2,1,0:T(8,128)(2,1)S(1)} %collective-permute-done.1), channel_id=1, source_target_pairs={{0,1},{1,2},{2,3},{3,4},{4,5},{5,6},{6,7},{7,0},{8,9},{9,10},{10,1... | collective-permute-start | bytes 393224 | tf_op jit(solution)/shard_map/ppermute | solution.py:22
  26.8 5.8 %collective-permute-start.5 = (bf16[1,16,32,128]{3,2,1,0:T(8,128)(2,1)S(1)}, bf16[1,16,32,128]{3,2,1,0:T(8,128)(2,1)S(1)}, u32[]{:S(2)}, u32[]{:S(2)}) collective-permute-start(bf16[1,16,32,128]{3,2,1,0:T(8,128)(2,1)S(1)} %collective-permute-done.4), channel_id=1, source_target_pairs={{1,0},{2,1},{3,2},{4,3},{5,4},{6,5},{7,6},{0,7},{9,8},{10,9},{11,1... | collective-permute-start | bytes 393224 | tf_op jit(solution)/shard_map/ppermute | solution.py:24
  32.3 6.2 %collective-permute-start.3 = (bf16[1,16,32,128]{3,2,1,0:T(8,128)(2,1)S(1)}, bf16[1,16,32,128]{3,2,1,0:T(8,128)(2,1)S(1)}, u32[]{:S(2)}, u32[]{:S(2)}) collective-permute-start(bf16[1,16,32,128]{3,2,1,0:T(8,128)(2,1)S(1)} %collective-permute-done.2), channel_id=1, source_target_pairs={{0,1},{1,2},{2,3},{3,4},{4,5},{5,6},{6,7},{7,0},{8,9},{9,10},{10,1... | collective-permute-start | bytes 393224 | tf_op jit(solution)/shard_map/ppermute | solution.py:22
  32.6 6.2 %collective-permute-start.6 = (bf16[1,16,32,128]{3,2,1,0:T(8,128)(2,1)S(1)}, bf16[1,16,32,128]{3,2,1,0:T(8,128)(2,1)S(1)}, u32[]{:S(2)}, u32[]{:S(2)}) collective-permute-start(bf16[1,16,32,128]{3,2,1,0:T(8,128)(2,1)S(1)} %collective-permute-done.5), channel_id=1, source_target_pairs={{1,0},{2,1},{3,2},{4,3},{5,4},{6,5},{7,6},{0,7},{9,8},{10,9},{11,1... | collective-permute-start | bytes 393224 | tf_op jit(solution)/shard_map/ppermute | solution.py:24
  80.1 101.3 %copy-start.1 = (f32[1,16,32,128]{3,2,1,0:T(8,128)S(1)}, f32[1,16,32,128]{3,2,1,0:T(8,128)}, u32[]{:S(2)}) copy-start(f32[1,16,32,128]{3,2,1,0:T(8,128)} %param.11) | copy-start | bytes 786436
  80.1 274.8 %reduce-scatter.6.cloned.1.call-start = ((), (), s32[]{:S(2)}) async-start(), calls=%async_computation.4 | async-start | bytes 8650752 | tf_op jit(solution)/shard_map/reduce_scatter | solution.py:59
  184.1 6.5 %collective-permute-start.7 = (bf16[1,16,32,128]{3,2,1,0:T(8,128)(2,1)S(1)}, bf16[1,16,32,128]{3,2,1,0:T(8,128)(2,1)S(1)}, u32[]{:S(2)}, u32[]{:S(2)}) collective-permute-start(bf16[1,16,32,128]{3,2,1,0:T(8,128)(2,1)S(1)} %convert_bitcast_fusion.1), channel_id=1, source_target_pairs={{0,1},{1,2},{2,3},{3,4},{4,5},{5,6},{6,7},{7,0},{8,9},{9,10},{10,1... | collective-permute-start | bytes 393224 | tf_op jit(solution)/shard_map/ppermute | solution.py:22
  190.6 6.6 %collective-permute-start.8 = (bf16[1,16,32,128]{3,2,1,0:T(8,128)(2,1)S(1)}, bf16[1,16,32,128]{3,2,1,0:T(8,128)(2,1)S(1)}, u32[]{:S(2)}, u32[]{:S(2)}) collective-permute-start(bf16[1,16,32,128]{3,2,1,0:T(8,128)(2,1)S(1)} %collective-permute-done.7), channel_id=1, source_target_pairs={{0,1},{1,2},{2,3},{3,4},{4,5},{5,6},{6,7},{7,0},{8,9},{9,10},{10,1... | collective-permute-start | bytes 393224 | tf_op jit(solution)/shard_map/ppermute | solution.py:22
  191.3 6.1 %collective-permute-start.11 = (bf16[1,16,32,128]{3,2,1,0:T(8,128)(2,1)S(1)}, bf16[1,16,32,128]{3,2,1,0:T(8,128)(2,1)S(1)}, u32[]{:S(2)}, u32[]{:S(2)}) collective-permute-start(bf16[1,16,32,128]{3,2,1,0:T(8,128)(2,1)S(1)} %convert_bitcast_fusion.1), channel_id=1, source_target_pairs={{1,0},{2,1},{3,2},{4,3},{5,4},{6,5},{7,6},{0,7},{9,8},{10,9},{11,1... | collective-permute-start | bytes 393224 | tf_op jit(solution)/shard_map/ppermute | solution.py:24
  197.2 7.4 %collective-permute-start.9 = (bf16[1,16,32,128]{3,2,1,0:T(8,128)(2,1)S(1)}, bf16[1,16,32,128]{3,2,1,0:T(8,128)(2,1)S(1)}, u32[]{:S(2)}, u32[]{:S(2)}) collective-permute-start(bf16[1,16,32,128]{3,2,1,0:T(8,128)(2,1)S(1)} %collective-permute-done.8), channel_id=1, source_target_pairs={{0,1},{1,2},{2,3},{3,4},{4,5},{5,6},{6,7},{7,0},{8,9},{9,10},{10,1... | collective-permute-start | bytes 393224 | tf_op jit(solution)/shard_map/ppermute | solution.py:22
  197.4 7.2 %collective-permute-start.12 = (bf16[1,16,32,128]{3,2,1,0:T(8,128)(2,1)S(1)}, bf16[1,16,32,128]{3,2,1,0:T(8,128)(2,1)S(1)}, u32[]{:S(2)}, u32[]{:S(2)}) collective-permute-start(bf16[1,16,32,128]{3,2,1,0:T(8,128)(2,1)S(1)} %collective-permute-done.11), channel_id=1, source_target_pairs={{1,0},{2,1},{3,2},{4,3},{5,4},{6,5},{7,6},{0,7},{9,8},{10,9},{11,1... | collective-permute-start | bytes 393224 | tf_op jit(solution)/shard_map/ppermute | solution.py:24
  204.6 6.2 %collective-permute-start.10 = (bf16[1,16,32,128]{3,2,1,0:T(8,128)(2,1)S(1)}, bf16[1,16,32,128]{3,2,1,0:T(8,128)(2,1)S(1)}, u32[]{:S(2)}, u32[]{:S(2)}) collective-permute-start(bf16[1,16,32,128]{3,2,1,0:T(8,128)(2,1)S(1)} %collective-permute-done.9), channel_id=1, source_target_pairs={{0,1},{1,2},{2,3},{3,4},{4,5},{5,6},{6,7},{7,0},{8,9},{9,10},{10,1... | collective-permute-start | bytes 393224 | tf_op jit(solution)/shard_map/ppermute | solution.py:22
  204.6 6.4 %collective-permute-start.13 = (bf16[1,16,32,128]{3,2,1,0:T(8,128)(2,1)S(1)}, bf16[1,16,32,128]{3,2,1,0:T(8,128)(2,1)S(1)}, u32[]{:S(2)}, u32[]{:S(2)}) collective-permute-start(bf16[1,16,32,128]{3,2,1,0:T(8,128)(2,1)S(1)} %collective-permute-done.12), channel_id=1, source_target_pairs={{1,0},{2,1},{3,2},{4,3},{5,4},{6,5},{7,6},{0,7},{9,8},{10,9},{11,1... | collective-permute-start | bytes 393224 | tf_op jit(solution)/shard_map/ppermute | solution.py:24
  211.0 1.0 copy-start.2
  254.6 273.7 %reduce-scatter.8.cloned.1.call-start = ((), (), s32[]{:S(2)}) async-start(), calls=%async_computation.5 | async-start | bytes 8650752 | tf_op jit(solution)/shard_map/reduce_scatter | solution.py:59
  357.7 6.3 %collective-permute-start.14 = (bf16[1,16,32,128]{3,2,1,0:T(8,128)(2,1)S(1)}, bf16[1,16,32,128]{3,2,1,0:T(8,128)(2,1)S(1)}, u32[]{:S(2)}, u32[]{:S(2)}) collective-permute-start(bf16[1,16,32,128]{3,2,1,0:T(8,128)(2,1)S(1)} %convert_bitcast_fusion), channel_id=1, source_target_pairs={{0,1},{1,2},{2,3},{3,4},{4,5},{5,6},{6,7},{7,0},{8,9},{9,10},{10,1... | collective-permute-start | bytes 393224 | tf_op jit(solution)/shard_map/ppermute | solution.py:22
  364.0 6.6 %collective-permute-start.15 = (bf16[1,16,32,128]{3,2,1,0:T(8,128)(2,1)S(1)}, bf16[1,16,32,128]{3,2,1,0:T(8,128)(2,1)S(1)}, u32[]{:S(2)}, u32[]{:S(2)}) collective-permute-start(bf16[1,16,32,128]{3,2,1,0:T(8,128)(2,1)S(1)} %collective-permute-done.14), channel_id=1, source_target_pairs={{0,1},{1,2},{2,3},{3,4},{4,5},{5,6},{6,7},{7,0},{8,9},{9,10},{10,1... | collective-permute-start | bytes 393224 | tf_op jit(solution)/shard_map/ppermute | solution.py:22
  364.7 6.1 %collective-permute-start.18 = (bf16[1,16,32,128]{3,2,1,0:T(8,128)(2,1)S(1)}, bf16[1,16,32,128]{3,2,1,0:T(8,128)(2,1)S(1)}, u32[]{:S(2)}, u32[]{:S(2)}) collective-permute-start(bf16[1,16,32,128]{3,2,1,0:T(8,128)(2,1)S(1)} %convert_bitcast_fusion), channel_id=1, source_target_pairs={{1,0},{2,1},{3,2},{4,3},{5,4},{6,5},{7,6},{0,7},{9,8},{10,9},{11,1... | collective-permute-start | bytes 393224 | tf_op jit(solution)/shard_map/ppermute | solution.py:24
  370.6 7.4 %collective-permute-start.16 = (bf16[1,16,32,128]{3,2,1,0:T(8,128)(2,1)S(1)}, bf16[1,16,32,128]{3,2,1,0:T(8,128)(2,1)S(1)}, u32[]{:S(2)}, u32[]{:S(2)}) collective-permute-start(bf16[1,16,32,128]{3,2,1,0:T(8,128)(2,1)S(1)} %collective-permute-done.15), channel_id=1, source_target_pairs={{0,1},{1,2},{2,3},{3,4},{4,5},{5,6},{6,7},{7,0},{8,9},{9,10},{10,1... | collective-permute-start | bytes 393224 | tf_op jit(solution)/shard_map/ppermute | solution.py:22
  370.8 7.2 %collective-permute-start.19 = (bf16[1,16,32,128]{3,2,1,0:T(8,128)(2,1)S(1)}, bf16[1,16,32,128]{3,2,1,0:T(8,128)(2,1)S(1)}, u32[]{:S(2)}, u32[]{:S(2)}) collective-permute-start(bf16[1,16,32,128]{3,2,1,0:T(8,128)(2,1)S(1)} %collective-permute-done.18), channel_id=1, source_target_pairs={{1,0},{2,1},{3,2},{4,3},{5,4},{6,5},{7,6},{0,7},{9,8},{10,9},{11,1... | collective-permute-start | bytes 393224 | tf_op jit(solution)/shard_map/ppermute | solution.py:24
  378.0 6.2 %collective-permute-start.17 = (bf16[1,16,32,128]{3,2,1,0:T(8,128)(2,1)S(1)}, bf16[1,16,32,128]{3,2,1,0:T(8,128)(2,1)S(1)}, u32[]{:S(2)}, u32[]{:S(2)}) collective-permute-start(bf16[1,16,32,128]{3,2,1,0:T(8,128)(2,1)S(1)} %collective-permute-done.16), channel_id=1, source_target_pairs={{0,1},{1,2},{2,3},{3,4},{4,5},{5,6},{6,7},{7,0},{8,9},{9,10},{10,1... | collective-permute-start | bytes 393224 | tf_op jit(solution)/shard_map/ppermute | solution.py:22
  378.0 6.4 %collective-permute-start.20 = (bf16[1,16,32,128]{3,2,1,0:T(8,128)(2,1)S(1)}, bf16[1,16,32,128]{3,2,1,0:T(8,128)(2,1)S(1)}, u32[]{:S(2)}, u32[]{:S(2)}) collective-permute-start(bf16[1,16,32,128]{3,2,1,0:T(8,128)(2,1)S(1)} %collective-permute-done.19), channel_id=1, source_target_pairs={{1,0},{2,1},{3,2},{4,3},{5,4},{6,5},{7,6},{0,7},{9,8},{10,9},{11,1... | collective-permute-start | bytes 393224 | tf_op jit(solution)/shard_map/ppermute | solution.py:24
  384.4 1.0 copy-start.3
Sparse Core Ops, SparseCore 0:
  80.3 101.0 reduce-scatter.3
  254.7 100.1 reduce-scatter.5
  428.1 100.1 reduce-scatter.7
